TPU v7x, 32 devices: a whole 2x2x4 slice. The times are simulated.
32 devices in a mesh: grp: 4 (over y, x), seq: 8 (over z, core).
Axes of the slice: x: 2, y: 2, z: 4, core: 2. Of those that a mesh axis runs over, the one named last changes fastest.
Arguments:
- queries: bfloat16 [1024, 64, 192], P('seq', 'grp'), may hold values from -6 to 6
- key_cache: bfloat16 [4, 8192, 192], P('grp', 'seq'), may hold values from -6 to 6
- group_value_cache: bfloat16 [4, 8192, 128], P('grp', 'seq'), may hold values from -6 to 6
- coarse_keys: bfloat16 [4, 512, 192], P('grp', 'seq'), may hold values from -6 to 6
- coarse_values: bfloat16 [4, 512, 128], P('grp', 'seq'), may hold values from -6 to 6
- hidden: bfloat16 [1024, 2560], P('seq'), may hold values from -6 to 6
- gate_weight: bfloat16 [4, 2560, 32], P('grp'), may hold values from -0.125 to 0.125
- out_weight: bfloat16 [8192, 2560], P('grp'), may hold values from -0.09375 to 0.09375
- selected: int32 [4, 8, 16], P('grp', 'seq'), may hold values from 0 to 127, as said below
Outputs:
- layer_out: bfloat16 [1024, 2560], P('seq', 'grp')
Inputs may be any that keep to these rules, and one draw needn't show every extreme that they name: selected[g, t] lists 16 distinct blocks of 64 positions for tile t of group g; the first is block 0; none starts after the tile's last query position; at most 4 of them lie within one index of seq's 1024 positions.
All inputs are finite; a program needn't handle non-finite values.
Results may differ from a plain program's by a relative error of at most 0.013.
Values may be sent and summed in bfloat16 or wider, within the bound.
A program may use at most 128 MiB of HBM per device.

v0:
```python
import math
import jax
import jax.numpy as jnp
from jax import lax
from jax.sharding import PartitionSpec as P

BLK = 64
SEL = 16
TILE = 128
CSTRIDE = 16
CLEN = 32
NEGATIVE = -1e30


def online_block(folded, part_keys, part_values, query_rows, row_pos, key_pos, score_scale):
    running, row_total, summed_out = folded
    logit_scores = (
        lax.dot_general(
            query_rows, part_keys, (((1,), (1,)), ((), ())), preferred_element_type=jnp.float32
        )
        * score_scale
    )
    logit_scores = jnp.where(key_pos[None, :] <= row_pos[:, None], logit_scores, -jnp.inf)
    new_max = jnp.maximum(running, jnp.max(logit_scores, axis=1))
    factor = jnp.exp(running - new_max)
    weights = jnp.exp(logit_scores - new_max[:, None])
    row_total = row_total * factor + jnp.sum(weights, axis=1)
    summed_out = summed_out * factor[:, None] + jnp.dot(
        weights.astype(jnp.bfloat16), part_values, preferred_element_type=jnp.float32
    )
    return (new_max, row_total, summed_out)


def shards(
    queries,
    key_cache,
    group_value_cache,
    coarse_keys,
    coarse_values,
    hidden,
    gate_weight,
    out_weight,
    selected,
):
    seq_count = lax.axis_size("seq")
    seq_index = lax.axis_index("seq")
    ctx_dev = key_cache.shape[1]
    context = ctx_dev * seq_count
    heads_here = queries.shape[1]
    key_width = queries.shape[2]
    value_width = group_value_cache.shape[2]
    score_scale = key_width ** (-0.5)
    query_rows = queries.reshape(TILE * heads_here, key_width)
    query_pos = context - TILE * seq_count + seq_index * TILE + jnp.arange(TILE, dtype=jnp.int32)
    row_pos = jnp.repeat(query_pos, heads_here)
    row_count = TILE * heads_here
    fold_start = (
        jnp.full((row_count,), NEGATIVE, jnp.float32),
        jnp.zeros((row_count,), jnp.float32),
        jnp.zeros((row_count, value_width), jnp.float32),
    )
    requests = lax.all_gather(selected[0], "seq", axis=0, tiled=True)
    blocks_dev = ctx_dev // BLK
    slot_cap = max(1, 2 * SEL // seq_count)
    owners = requests // blocks_dev
    earlier = jnp.tril(jnp.ones((SEL, SEL), jnp.int32), -1)
    same_owner = (owners[:, :, None] == owners[:, None, :]).astype(jnp.int32)
    order_rank = jnp.sum(same_owner * earlier[None], axis=2)
    served = owners == seq_index
    slot_ids = jnp.arange(slot_cap, dtype=jnp.int32)
    matches = (served[:, :, None] & (order_rank[:, :, None] == slot_ids[None, None, :])).astype(
        jnp.int32
    )
    local_block = jnp.sum(matches * (requests - seq_index * blocks_dev)[:, :, None], axis=1)
    filled = jnp.sum(matches, axis=1) > 0
    block_keys_grouped = key_cache[0].reshape(blocks_dev, BLK, key_width)
    value_blocks = group_value_cache[0].reshape(blocks_dev, BLK, value_width)
    outgoing = jnp.concatenate(
        [
            jnp.take(block_keys_grouped, local_block, axis=0),
            jnp.take(value_blocks, local_block, axis=0),
        ],
        axis=3,
    )
    outgoing = jnp.where(filled[:, :, None, None], outgoing, jnp.zeros_like(outgoing))
    incoming = lax.all_to_all(outgoing, "seq", split_axis=0, concat_axis=0, tiled=True)
    piece_keys = lax.all_gather(coarse_keys[0], "seq", axis=0, tiled=True)
    piece_values = lax.all_gather(coarse_values[0], "seq", axis=0, tiled=True)
    length = piece_keys.shape[0]
    span_rows = math.gcd(length, 512)

    def advance(loop_index, state_now):
        offset = loop_index * span_rows
        part_keys = lax.dynamic_slice_in_dim(piece_keys, offset, span_rows, 0)
        part_values = lax.dynamic_slice_in_dim(piece_values, offset, span_rows, 0)
        key_pos = (offset + jnp.arange(span_rows, dtype=jnp.int32)) * CSTRIDE + CLEN - 1
        return online_block(
            state_now, part_keys, part_values, query_rows, row_pos, key_pos, score_scale
        )

    coarse_state = lax.fori_loop(0, length // span_rows, advance, fold_start)
    coarse_out = coarse_state[2] / coarse_state[1][:, None]
    own_list = selected[0, 0]
    own_owner = own_list // blocks_dev
    own_rank = jnp.sum(
        (own_owner[:, None] == own_owner[None, :]).astype(jnp.int32) * earlier, axis=1
    )
    picked_rows = incoming[own_owner, own_rank].reshape(SEL * BLK, key_width + value_width)
    picked_keys = picked_rows[:, :key_width]
    picked_values = picked_rows[:, key_width:]
    picked_pos = (own_list[:, None] * BLK + jnp.arange(BLK, dtype=jnp.int32)[None, :]).reshape(-1)
    picked_state = online_block(
        fold_start, picked_keys, picked_values, query_rows, row_pos, picked_pos, score_scale
    )
    picked_out = picked_state[2] / picked_state[1][:, None]
    gate_logits = jnp.dot(hidden, gate_weight[0], preferred_element_type=jnp.float32)
    gate_coarse = jax.nn.sigmoid(gate_logits[:, :heads_here])
    gate_picked = jax.nn.sigmoid(gate_logits[:, heads_here:])
    mixed_heads = gate_coarse[:, :, None] * coarse_out.reshape(
        TILE, heads_here, value_width
    ) + gate_picked[:, :, None] * picked_out.reshape(TILE, heads_here, value_width)
    attended = mixed_heads.astype(jnp.bfloat16).reshape(TILE, heads_here * value_width)
    partial_value = jnp.dot(attended, out_weight, preferred_element_type=jnp.float32)
    result = lax.psum_scatter(
        partial_value.astype(jnp.bfloat16), "grp", scatter_dimension=1, tiled=True
    )
    return result


def solution(mesh):
    return jax.shard_map(
        shards,
        mesh=mesh,
        in_specs=(
            P("seq", "grp", None),
            P("grp", "seq", None),
            P("grp", "seq", None),
            P("grp", "seq", None),
            P("grp", "seq", None),
            P("seq", None),
            P("grp", None, None),
            P("grp", None),
            P("grp", "seq", None),
        ),
        out_specs=P("seq", "grp"),
        check_vma=False,
    )
```

profile of v0, /device:TPU:0, one launch (start us, length us, event | category | flops | bytes accessed | tf_op | source)
XLA Modules:
  0.0 154.2 jit_solution(9140498446499711631)
XLA Ops:
  6.5 13.7 %all-gather.2 = s32[8,1,16]{2,1,0:T(1,128)S(1)} all-gather(s32[1,1,16]{2,1,0:T(1,128)} %param.17), channel_id=4, replica_groups=mesh['grp'=4,'seq'=8] {'seq'}, dimensions={0}, use_global_device_ids=true | all-gather | bytes 576 | tf_op jit(solution)/shard_map/all_gather | solution.py:62
  20.3 0.7 bitcast_multiply_fusion.2
  21.0 0.2 select_reduce_fusion.2
  21.2 0.3 select_reduce_fusion
  21.5 0.2 convert_reduce_fusion
  22.0 1.2 copy.40
  23.2 0.6 gather_fusion
  23.8 1.6 %gather_fusion.1 = bf16[32,64,128]{2,1,0:T(8,128)(2,1)S(1)} fusion(bf16[16,64,128]{2,1,0:T(8,128)(2,1)} %bitcast.90, s32[1024]{0:T(1024)S(1)} %pad_clamp_fusion), kind=kCustom, calls=%fused_computation.1 | custom fusion | bytes 1048704 | tf_op jit(solution)/shard_map/jit(_take)/gather | solution.py:81
  25.4 0.2 broadcast_select_fusion
  25.6 0.1 broadcast_select_fusion.1
  25.8 1.9 %maximum_select_fusion = bf16[8,4,64,320]{3,2,1,0:T(8,128)(2,1)} fusion(bf16[8,4,64,128]{3,2,1,0:T(8,128)(2,1)S(1)} %broadcast_select_fusion.1, bf16[8,4,64,192]{3,2,1,0:T(8,128)(2,1)S(1)} %broadcast_select_fusion, pred[8,4]{1,0:T(8,128)(4,1)S(1)} %copy.38), kind=kLoop, calls=%fused_computation.20 | loop fusion | flops 3276800 | bytes 2621472 | tf_op jit(solution)/shard_map/jit(_where)/select_n | solution.py:85
  27.7 3.6 %all-to-all-start = ((bf16[8,4,64,320]{3,2,1,0:T(8,128)(2,1)}), bf16[8,4,64,320]{3,2,1,0:T(8,128)(2,1)S(1)}, u32[]{:S(2)}, u32[]{:S(2)}) async-start(bf16[8,4,64,320]{3,2,1,0:T(8,128)(2,1)} %maximum_select_fusion), calls=%async_computation | async-start | bytes 3145728 | tf_op jit(solution)/shard_map/all_to_all | solution.py:86
  31.5 45.0 %all-gather.1 = bf16[1,512,128]{2,1,0:T(8,128)(2,1)} all-gather(bf16[1,64,128]{2,1,0:T(8,128)(2,1)S(1)} %copy-done.5), channel_id=3, replica_groups=mesh['grp'=4,'seq'=8] {'seq'}, dimensions={1}, use_global_device_ids=true | all-gather | bytes 147456 | tf_op jit(solution)/shard_map/all_gather | solution.py:88
  76.7 1.8 %copy.36 = bf16[128,16,192]{2,1,0:T(8,128)(2,1)S(1)} copy(bf16[128,16,192]{0,2,1:T(8,128)(2,1)} %param.9) | data formatting | bytes 1572864 | tf_op args[0]
  78.6 14.4 %all-gather = bf16[1,512,192]{2,1,0:T(8,128)(2,1)S(1)} all-gather(bf16[1,64,192]{2,1,0:T(8,128)(2,1)S(1)} %copy-done.4), channel_id=2, replica_groups=mesh['grp'=4,'seq'=8] {'seq'}, dimensions={1}, use_global_device_ids=true | all-gather | bytes 221184 | tf_op jit(solution)/shard_map/all_gather | solution.py:87
  92.9 0.8 fusion.47
  93.8 0.6 fusion.6
  94.4 0.2 copy-done.3
  94.6 2.1 %fusion.8 = f32[2048,128]{1,0:T(8,128)} fusion(f32[2048,512]{0,1:T(8,128)S(1)} %get-tuple-element.49, f32[2048]{0:T(1024)S(1)} %broadcast_maximum_fusion.1, f32[2048]{0:T(1024)S(1)} %get-tuple-element.38, f32[2048]{0:T(1024)S(1)} %get-tuple-element.36, bf16[1,512,128]{2,1,0:T(8,128)(2,1)S(1)} %copy-done.3), kind=kOutput, calls=%fused_computation.16 | convolution fusion | flops 271056896 | bytes 5398528 | tf_op jit(solution)/shard_map/while/body/eval_jaxpr/dot_general | solution.py:28
  96.7 1.4 reshape.242
  98.1 0.3 fusion.24
  98.7 1.5 %gather_fusion.2 = bf16[16,64,320]{2,1,0:T(8,128)(2,1)} fusion(bf16[8,4,64,320]{3,2,1,0:T(8,128)(2,1)S(1)} %all-to-all-done, s32[16]{0:T(128)S(1)} %fusion.42), kind=kCustom, calls=%fused_computation.2 | custom fusion | bytes 1310848 | tf_op jit(solution)/shard_map/gather | solution.py:108
  100.2 2.7 %fusion.2 = (f32[2048]{0:T(1024)S(1)}, f32[1024,2048]{1,0:T(8,128)S(1)}) fusion(s32[2048]{0:T(1024)S(1)} %le.51, s32[1024]{0:T(1024)S(1)} %add.162, bf16[2048,192]{1,0:T(8,128)(2,1)} %bitcast.89, bf16[1024,320]{1,0:T(8,128)(2,1)} %bitcast.91), kind=kOutput, calls=%fused_computation.7 | convolution fusion | flops 813692928 | bytes 9981952 | tf_op jit(solution)/shard_map/dot_general | solution.py:18
  103.0 2.4 %fusion = f32[2048]{0:T(1024)S(1)} fusion(f32[1024,2048]{1,0:T(8,128)S(1)} %get-tuple-element.47, f32[2048]{0:T(1024)S(1)} %broadcast_maximum_fusion, s32[2048]{0:T(1024)S(1)} %le.51, s32[1024]{0:T(1024)S(1)} %add.162), kind=kLoop, calls=%fused_computation.5 | loop fusion | flops 10483712 | bytes 8417280 | tf_op jit(solution)/shard_map/reduce_sum | solution.py:27
  105.4 4.6 %fusion.14 = f32[2048,128]{1,0:T(8,128)} fusion(f32[1024,2048]{1,0:T(8,128)S(1)} %get-tuple-element.47, f32[2048]{0:T(1024)S(1)} %broadcast_maximum_fusion, s32[2048]{0:T(1024)S(1)} %le.51, s32[1024]{0:T(1024)S(1)} %add.162, f32[2048]{0:T(1024)S(1)} %get-tuple-element.41, f32[2048]{0:T(1024)S(1)} %get-tuple-element.40, bf16[1024,320]{1,0:T(8,128)(2,1)} %bitcast.92), kind=kOutput, calls=%fused_computation.19 | convolution fusion | flops 547880960 | bytes 9736192 | tf_op jit(solution)/shard_map/dot_general | solution.py:28
  110.0 1.4 reshape.244
  111.4 0.3 mul.102
  111.8 0.3 mul.110
  112.1 6.3 %convolution_convert_fusion = bf16[128,2560]{1,0:T(8,128)(2,1)S(1)} fusion(bf16[2048,2560]{1,0:T(8,128)(2,1)} %param.16, f32[128,2048]{1,0:T(8,128)S(1)} %reshape.244, f32[16,8,16,128]{3,2,1,0:T(8,128)S(1)} %bitcast.83, f32[128,2048]{1,0:T(8,128)S(1)} %reshape.242, f32[16,8,16,128]{3,2,1,0:T(8,128)S(1)} %bitcast.82), kind=kOutput, calls=%fused_computation.14 | convolution fusion | flops 1343553536 | bytes 15335424 | tf_op jit(solution)/shard_map/dot_general | solution.py:123
  118.4 1.1 copy.43
  119.5 26.1 %reduce-scatter.4.cloned.1.call-done = bf16[640,128]{1,0:T(8,128)(2,1)} async-done(((bf16[2560,128]{1,0:T(8,128)(2,1)}), bf16[640,128]{1,0:T(8,128)(2,1)}) %reduce-scatter.4.cloned.1.call-update) | async-done | bytes 163856
  145.6 1.7 %copy.44 = bf16[128,640]{1,0:T(8,128)(2,1)} copy(bf16[128,640]{0,1:T(8,128)(2,1)} %bitcast.93) | data formatting | bytes 327680
  (40 shorter events, 1.1 us)
Async XLA Ops:
  6.5 91.6 %copy-start = (bf16[128,2560]{1,0:T(8,128)(2,1)S(1)}, bf16[128,2560]{1,0:T(8,128)(2,1)}, u32[]{:S(2)}) copy-start(bf16[128,2560]{1,0:T(8,128)(2,1)} %param.14) | copy-start | bytes 1966084
  25.6 5.9 %copy-start.5 = (bf16[1,64,128]{2,1,0:T(8,128)(2,1)S(1)}, bf16[1,64,128]{2,1,0:T(8,128)(2,1)}, u32[]{:S(2)}) copy-start(bf16[1,64,128]{2,1,0:T(8,128)(2,1)} %param.13) | copy-start | bytes 49156
  25.8 52.7 %copy-start.4 = (bf16[1,64,192]{2,1,0:T(8,128)(2,1)S(1)}, bf16[1,64,192]{2,1,0:T(8,128)(2,1)}, u32[]{:S(2)}) copy-start(bf16[1,64,192]{2,1,0:T(8,128)(2,1)} %param.12) | copy-start | bytes 73732
  27.7 71.0 %all-to-all-start = ((bf16[8,4,64,320]{3,2,1,0:T(8,128)(2,1)}), bf16[8,4,64,320]{3,2,1,0:T(8,128)(2,1)S(1)}, u32[]{:S(2)}, u32[]{:S(2)}) async-start(bf16[8,4,64,320]{3,2,1,0:T(8,128)(2,1)} %maximum_select_fusion), calls=%async_computation | async-start | bytes 3145728 | tf_op jit(solution)/shard_map/all_to_all | solution.py:86
  31.3 114.3 %reduce-scatter.4.cloned.1.call-start = ((), (), s32[]{:S(2)}) async-start(), calls=%async_computation.2 | async-start | bytes 819200
  78.5 15.9 %copy-start.1 = (bf16[128,16,192]{2,1,0:T(8,128)(2,1)}, bf16[128,16,192]{2,1,0:T(8,128)(2,1)S(1)}, u32[]{:S(2)}) copy-start(bf16[128,16,192]{2,1,0:T(8,128)(2,1)S(1)} %copy.36) | copy-start | bytes 2359300
  93.7 0.9 copy-start.3
  94.6 3.5 %copy-start.2 = (bf16[1,2560,32]{1,2,0:T(8,128)(2,1)S(1)}, bf16[1,2560,32]{1,2,0:T(8,128)(2,1)}, u32[]{:S(2)}) copy-start(bf16[1,2560,32]{1,2,0:T(8,128)(2,1)} %param.15) | copy-start | bytes 491524
  94.6 4.0 %copy-start.6 = (s32[1,1,16]{2,1,0:T(1,128)S(1)}, s32[1,1,16]{2,1,0:T(1,128)}, u32[]{:S(2)}) copy-start(s32[1,1,16]{2,1,0:T(1,128)} %param.17) | copy-start | bytes 196
Sparse Core Ops, SparseCore 0:
  119.7 25.9 reduce-scatter.3
where the time goes:
time: 155 us; the launch traced here: 154 us
  blocking collectives  73.1 us (47%)
  waiting for transfers between devices  26.1 us (17%)
  matrix products  16.8 us (11%)
  local copies, waits for them, and re-layouts  14 us (9%)
  between operations  13.7 us (9%)
  other arithmetic  6.8 us (4%)
  starting transfers between devices  3.62 us (2%)
    all_gather x1, blocking collectives, shards(): piece_values = lax.all_gather(coarse_values[0], 'seq', axis=0, tiled=True)  45 us
    unnamed x2, waiting for transfers between devices  26.1 us
    all_gather x1, blocking collectives, shards(): piece_keys = lax.all_gather(coarse_keys[0], 'seq', axis=0, tiled=True)  14.4 us
    all_gather x1, blocking collectives, shards(): requests = lax.all_gather(selected[0], 'seq', axis=0, tiled=True)  13.7 us
    dot_general x2, matrix products, online_block(): jnp.dot(weights.astype(jnp.bfloat16), part_values, preferred_element_type...  6.69 us
    dot_general x1, matrix products, shards(): jnp.dot(attended, out_weight, preferred_element_type=jnp.float32)  6.32 us
    unnamed x18, local copies, waits for them, and re-layouts  6.06 us
    all_to_all x1, starting transfers between devices, shards(): lax.all_to_all(outgoing, 'seq', split_axis=0, concat_axis=0, tiled=True)  3.58 us
  transfers between devices with their start and end apart: 2, of which 1 were waited for; matrix products, arithmetic and copies ran while one was open for 5% of the time, Pallas kernels for 0%

commit v1 on v0

--- a/solution.py
+++ b/solution.py
@@ -59,7 +59,15 @@
         jnp.zeros((row_count,), jnp.float32),
         jnp.zeros((row_count, value_width), jnp.float32),
     )
-    requests = lax.all_gather(selected[0], "seq", axis=0, tiled=True)
+    own = selected[0]
+    size = lax.axis_size("seq")
+    route = [(i, (i + 1) % size) for i in range(size)]
+    terms = [own]
+    for far in range(1, size):
+        terms = [lax.ppermute(terms[0], "seq", route), *terms]
+    result_2 = jnp.concatenate(terms, axis=0)
+    shift = (lax.axis_index("seq") + 1) * terms[-1].shape[0]
+    requests = jnp.roll(result_2, shift, axis=0)
     blocks_dev = ctx_dev // BLK
     slot_cap = max(1, 2 * SEL // seq_count)
     owners = requests // blocks_dev

time: 155 us -> 175 us (1.13)
  waiting for transfers between devices: 26.1 us -> 58.6 us
  blocking collectives: 73.1 us -> 59.5 us
    ppermute x0 -> x7, waiting for transfers between devices: none -> 32 us  [shards(): terms = [lax.ppermute(terms[0], 'seq', route), *terms]]
    all_gather x1 -> x0, blocking collectives: 13.7 us -> none  [shards(): requests = lax.all_gather(selected[0], 'seq', axis=0, tiled=True)]
  transfers between devices with their start and end apart: 2 -> 9, of which waited for: 1 -> 8; matrix products, arithmetic and copies ran while one was open for 5% -> 5% of each run, Pallas kernels for 0% -> 0%
where the time goes in v1:
time: 175 us
  blocking collectives  59.5 us (34%)
  waiting for transfers between devices  58.6 us (33%)
  matrix products  16.8 us (10%)
  local copies, waits for them, and re-layouts  15.4 us (9%)
  between operations  13.7 us (8%)
  other arithmetic  6.83 us (4%)
  starting transfers between devices  4.13 us (2%)
    all_gather x1, blocking collectives, shards(): piece_values = lax.all_gather(coarse_values[0], 'seq', axis=0, tiled=True)  45.1 us
    ppermute x7, waiting for transfers between devices, shards(): terms = [lax.ppermute(terms[0], 'seq', route), *terms]  32 us
    unnamed x2, waiting for transfers between devices  26.6 us
    all_gather x1, blocking collectives, shards(): piece_keys = lax.all_gather(coarse_keys[0], 'seq', axis=0, tiled=True)  14.4 us
    dot_general x2, matrix products, online_block(): jnp.dot(weights.astype(jnp.bfloat16), part_values, preferred_element_type...  6.68 us
    dot_general x1, matrix products, shards(): jnp.dot(attended, out_weight, preferred_element_type=jnp.float32)  6.33 us
    unnamed x18, local copies, waits for them, and re-layouts  6.06 us
    all_to_all x1, starting transfers between devices, shards(): lax.all_to_all(outgoing, 'seq', split_axis=0, concat_axis=0, tiled=True)  3.58 us
  transfers between devices with their start and end apart: 9, of which 8 were waited for; matrix products, arithmetic and copies ran while one was open for 5% of the time, Pallas kernels for 0%

profile of v1, /device:TPU:0, one launch (start us, length us, event | category | flops | bytes accessed | tf_op | source)
XLA Modules:
  0.0 174.9 jit_solution(14104723052976343747)
XLA Ops:
  6.5 0.5 collective-permute-start
  7.0 0.7 bitcast_multiply_fusion.2
  8.0 4.5 %collective-permute-done = s32[1,16]{1,0:T(1,128)S(1)} collective-permute-done((s32[1,16]{1,0:T(1,128)}, s32[1,16]{1,0:T(1,128)S(1)}, u32[]{:S(2)}, u32[]{:S(2)}) %collective-permute-start) | collective-permute-done | bytes 96 | tf_op jit(solution)/shard_map/ppermute | solution.py:67
  12.4 4.8 %collective-permute-done.1 = s32[1,16]{1,0:T(1,128)S(1)} collective-permute-done((s32[1,16]{1,0:T(1,128)S(1)}, s32[1,16]{1,0:T(1,128)S(1)}, u32[]{:S(2)}, u32[]{:S(2)}) %collective-permute-start.1) | collective-permute-done | bytes 96 | tf_op jit(solution)/shard_map/ppermute | solution.py:67
  17.2 4.8 %collective-permute-done.2 = s32[1,16]{1,0:T(1,128)S(1)} collective-permute-done((s32[1,16]{1,0:T(1,128)S(1)}, s32[1,16]{1,0:T(1,128)S(1)}, u32[]{:S(2)}, u32[]{:S(2)}) %collective-permute-start.2) | collective-permute-done | bytes 96 | tf_op jit(solution)/shard_map/ppermute | solution.py:67
  22.0 4.8 %collective-permute-done.3 = s32[1,16]{1,0:T(1,128)S(1)} collective-permute-done((s32[1,16]{1,0:T(1,128)S(1)}, s32[1,16]{1,0:T(1,128)S(1)}, u32[]{:S(2)}, u32[]{:S(2)}) %collective-permute-start.3) | collective-permute-done | bytes 96 | tf_op jit(solution)/shard_map/ppermute | solution.py:67
  26.8 4.8 %collective-permute-done.4 = s32[1,16]{1,0:T(1,128)S(1)} collective-permute-done((s32[1,16]{1,0:T(1,128)S(1)}, s32[1,16]{1,0:T(1,128)S(1)}, u32[]{:S(2)}, u32[]{:S(2)}) %collective-permute-start.4) | collective-permute-done | bytes 96 | tf_op jit(solution)/shard_map/ppermute | solution.py:67
  31.6 1.2 copy.38
  32.8 3.6 %collective-permute-done.5 = s32[1,16]{1,0:T(1,128)S(1)} collective-permute-done((s32[1,16]{1,0:T(1,128)S(1)}, s32[1,16]{1,0:T(1,128)S(1)}, u32[]{:S(2)}, u32[]{:S(2)}) %collective-permute-start.5) | collective-permute-done | bytes 96 | tf_op jit(solution)/shard_map/ppermute | solution.py:67
  36.4 4.8 %collective-permute-done.6 = s32[1,16]{1,0:T(1,128)S(1)} collective-permute-done((s32[1,16]{1,0:T(1,128)S(1)}, s32[1,16]{1,0:T(1,128)S(1)}, u32[]{:S(2)}, u32[]{:S(2)}) %collective-permute-start.6) | collective-permute-done | bytes 96 | tf_op jit(solution)/shard_map/ppermute | solution.py:67
  41.2 1.4 concatenate.12
  43.4 0.6 gather_fusion
  44.0 1.6 gather_fusion.1
  46.0 1.9 %maximum_select_fusion = bf16[8,4,64,320]{3,2,1,0:T(8,128)(2,1)} fusion(bf16[8,4,64,128]{3,2,1,0:T(8,128)(2,1)S(1)} %broadcast_select_fusion.1, bf16[8,4,64,192]{3,2,1,0:T(8,128)(2,1)S(1)} %broadcast_select_fusion, pred[8,4]{1,0:T(8,128)(4,1)S(1)} %copy.36), kind=kLoop, calls=%fused_computation.20 | loop fusion | flops 3276800 | bytes 2621472 | tf_op jit(solution)/shard_map/jit(_where)/select_n | solution.py:93
  48.0 3.6 %all-to-all-start = ((bf16[8,4,64,320]{3,2,1,0:T(8,128)(2,1)}), bf16[8,4,64,320]{3,2,1,0:T(8,128)(2,1)S(1)}, u32[]{:S(2)}, u32[]{:S(2)}) async-start(bf16[8,4,64,320]{3,2,1,0:T(8,128)(2,1)} %maximum_select_fusion), calls=%async_computation | async-start | bytes 3145728 | tf_op jit(solution)/shard_map/all_to_all | solution.py:94
  51.6 45.1 %all-gather.1 = bf16[1,512,128]{2,1,0:T(8,128)(2,1)} all-gather(bf16[1,64,128]{2,1,0:T(8,128)(2,1)S(1)} %copy-done.5), channel_id=3, replica_groups=mesh['grp'=4,'seq'=8] {'seq'}, dimensions={1}, use_global_device_ids=true | all-gather | bytes 147456 | tf_op jit(solution)/shard_map/all_gather | solution.py:96
  97.0 1.8 %copy.34 = bf16[128,16,192]{2,1,0:T(8,128)(2,1)S(1)} copy(bf16[128,16,192]{0,2,1:T(8,128)(2,1)} %param.9) | data formatting | bytes 1572864 | tf_op args[0]
  98.8 14.4 %all-gather = bf16[1,512,192]{2,1,0:T(8,128)(2,1)S(1)} all-gather(bf16[1,64,192]{2,1,0:T(8,128)(2,1)S(1)} %copy-done.4), channel_id=2, replica_groups=mesh['grp'=4,'seq'=8] {'seq'}, dimensions={1}, use_global_device_ids=true | all-gather | bytes 221184 | tf_op jit(solution)/shard_map/all_gather | solution.py:95
  113.2 0.8 fusion.47
  114.0 0.6 fusion.6
  114.9 2.1 %fusion.8 = f32[2048,128]{1,0:T(8,128)} fusion(f32[2048,512]{0,1:T(8,128)S(1)} %get-tuple-element.49, f32[2048]{0:T(1024)S(1)} %broadcast_maximum_fusion.1, f32[2048]{0:T(1024)S(1)} %get-tuple-element.38, f32[2048]{0:T(1024)S(1)} %get-tuple-element.36, bf16[1,512,128]{2,1,0:T(8,128)(2,1)S(1)} %copy-done.3), kind=kOutput, calls=%fused_computation.16 | convolution fusion | flops 271056896 | bytes 5398528 | tf_op jit(solution)/shard_map/while/body/eval_jaxpr/dot_general | solution.py:28
  117.0 1.4 reshape.242
  118.9 1.5 gather_fusion.2
  120.5 2.7 %fusion.2 = (f32[2048]{0:T(1024)S(1)}, f32[1024,2048]{1,0:T(8,128)S(1)}) fusion(s32[2048]{0:T(1024)S(1)} %le.51, s32[1024]{0:T(1024)S(1)} %add.175, bf16[2048,192]{1,0:T(8,128)(2,1)} %bitcast.89, bf16[1024,320]{1,0:T(8,128)(2,1)} %bitcast.91), kind=kOutput, calls=%fused_computation.7 | convolution fusion | flops 813692928 | bytes 9981952 | tf_op jit(solution)/shard_map/dot_general | solution.py:18
  123.2 2.4 %fusion = f32[2048]{0:T(1024)S(1)} fusion(f32[1024,2048]{1,0:T(8,128)S(1)} %get-tuple-element.47, f32[2048]{0:T(1024)S(1)} %broadcast_maximum_fusion, s32[2048]{0:T(1024)S(1)} %le.51, s32[1024]{0:T(1024)S(1)} %add.175), kind=kLoop, calls=%fused_computation.5 | loop fusion | flops 10483712 | bytes 8417280 | tf_op jit(solution)/shard_map/reduce_sum | solution.py:27
  125.7 4.6 %fusion.14 = f32[2048,128]{1,0:T(8,128)} fusion(f32[1024,2048]{1,0:T(8,128)S(1)} %get-tuple-element.47, f32[2048]{0:T(1024)S(1)} %broadcast_maximum_fusion, s32[2048]{0:T(1024)S(1)} %le.51, s32[1024]{0:T(1024)S(1)} %add.175, f32[2048]{0:T(1024)S(1)} %get-tuple-element.41, f32[2048]{0:T(1024)S(1)} %get-tuple-element.40, bf16[1024,320]{1,0:T(8,128)(2,1)} %bitcast.92), kind=kOutput, calls=%fused_computation.19 | convolution fusion | flops 547880960 | bytes 9736192 | tf_op jit(solution)/shard_map/dot_general | solution.py:28
  130.3 1.4 reshape.244
  132.0 0.3 mul.110
  132.3 6.3 %convolution_convert_fusion = bf16[128,2560]{1,0:T(8,128)(2,1)S(1)} fusion(bf16[2048,2560]{1,0:T(8,128)(2,1)} %param.16, f32[128,2048]{1,0:T(8,128)S(1)} %reshape.244, f32[16,8,16,128]{3,2,1,0:T(8,128)S(1)} %bitcast.83, f32[128,2048]{1,0:T(8,128)S(1)} %reshape.242, f32[16,8,16,128]{3,2,1,0:T(8,128)S(1)} %bitcast.82), kind=kOutput, calls=%fused_computation.14 | convolution fusion | flops 1343553536 | bytes 15335424 | tf_op jit(solution)/shard_map/dot_general | solution.py:131
  138.6 1.1 copy.41
  139.8 26.6 %reduce-scatter.4.cloned.1.call-done = bf16[640,128]{1,0:T(8,128)(2,1)} async-done(((bf16[2560,128]{1,0:T(8,128)(2,1)}), bf16[640,128]{1,0:T(8,128)(2,1)}) %reduce-scatter.4.cloned.1.call-update) | async-done | bytes 163856
  166.3 1.7 copy.42
  (54 shorter events, 2.9 us)
Async XLA Ops:
  6.5 111.8 %copy-start = (bf16[128,2560]{1,0:T(8,128)(2,1)S(1)}, bf16[128,2560]{1,0:T(8,128)(2,1)}, u32[]{:S(2)}) copy-start(bf16[128,2560]{1,0:T(8,128)(2,1)} %param.14) | copy-start | bytes 1966084
  6.5 5.9 %collective-permute-start = (s32[1,16]{1,0:T(1,128)}, s32[1,16]{1,0:T(1,128)S(1)}, u32[]{:S(2)}, u32[]{:S(2)}) collective-permute-start(s32[1,16]{1,0:T(1,128)} %bitcast.94), channel_id=1, source_target_pairs={{0,1},{1,2},{2,3},{3,4},{4,5},{5,6},{6,7},{7,0},{8,9},{9,10},{10,1... | collective-permute-start | bytes 200 | tf_op jit(solution)/shard_map/ppermute | solution.py:67
  12.4 4.8 %collective-permute-start.1 = (s32[1,16]{1,0:T(1,128)S(1)}, s32[1,16]{1,0:T(1,128)S(1)}, u32[]{:S(2)}, u32[]{:S(2)}) collective-permute-start(s32[1,16]{1,0:T(1,128)S(1)} %collective-permute-done), channel_id=1, source_target_pairs={{0,1},{1,2},{2,3},{3,4},{4,5},{5,6},{6,7},{7,0},{8,9},{9,10},{10,1... | collective-permute-start | bytes 200 | tf_op jit(solution)/shard_map/ppermute | solution.py:67
  17.2 4.8 %collective-permute-start.2 = (s32[1,16]{1,0:T(1,128)S(1)}, s32[1,16]{1,0:T(1,128)S(1)}, u32[]{:S(2)}, u32[]{:S(2)}) collective-permute-start(s32[1,16]{1,0:T(1,128)S(1)} %collective-permute-done.1), channel_id=1, source_target_pairs={{0,1},{1,2},{2,3},{3,4},{4,5},{5,6},{6,7},{7,0},{8,9},{9,10},{10,1... | collective-permute-start | bytes 200 | tf_op jit(solution)/shard_map/ppermute | solution.py:67
  22.0 4.8 %collective-permute-start.3 = (s32[1,16]{1,0:T(1,128)S(1)}, s32[1,16]{1,0:T(1,128)S(1)}, u32[]{:S(2)}, u32[]{:S(2)}) collective-permute-start(s32[1,16]{1,0:T(1,128)S(1)} %collective-permute-done.2), channel_id=1, source_target_pairs={{0,1},{1,2},{2,3},{3,4},{4,5},{5,6},{6,7},{7,0},{8,9},{9,10},{10,1... | collective-permute-start | bytes 200 | tf_op jit(solution)/shard_map/ppermute | solution.py:67
  26.8 4.8 %collective-permute-start.4 = (s32[1,16]{1,0:T(1,128)S(1)}, s32[1,16]{1,0:T(1,128)S(1)}, u32[]{:S(2)}, u32[]{:S(2)}) collective-permute-start(s32[1,16]{1,0:T(1,128)S(1)} %collective-permute-done.3), channel_id=1, source_target_pairs={{0,1},{1,2},{2,3},{3,4},{4,5},{5,6},{6,7},{7,0},{8,9},{9,10},{10,1... | collective-permute-start | bytes 200 | tf_op jit(solution)/shard_map/ppermute | solution.py:67
  31.6 4.8 %collective-permute-start.5 = (s32[1,16]{1,0:T(1,128)S(1)}, s32[1,16]{1,0:T(1,128)S(1)}, u32[]{:S(2)}, u32[]{:S(2)}) collective-permute-start(s32[1,16]{1,0:T(1,128)S(1)} %collective-permute-done.4), channel_id=1, source_target_pairs={{0,1},{1,2},{2,3},{3,4},{4,5},{5,6},{6,7},{7,0},{8,9},{9,10},{10,1... | collective-permute-start | bytes 200 | tf_op jit(solution)/shard_map/ppermute | solution.py:67
  36.4 4.8 %collective-permute-start.6 = (s32[1,16]{1,0:T(1,128)S(1)}, s32[1,16]{1,0:T(1,128)S(1)}, u32[]{:S(2)}, u32[]{:S(2)}) collective-permute-start(s32[1,16]{1,0:T(1,128)S(1)} %collective-permute-done.5), channel_id=1, source_target_pairs={{0,1},{1,2},{2,3},{3,4},{4,5},{5,6},{6,7},{7,0},{8,9},{9,10},{10,1... | collective-permute-start | bytes 200 | tf_op jit(solution)/shard_map/ppermute | solution.py:67
  45.8 5.8 %copy-start.5 = (bf16[1,64,128]{2,1,0:T(8,128)(2,1)S(1)}, bf16[1,64,128]{2,1,0:T(8,128)(2,1)}, u32[]{:S(2)}) copy-start(bf16[1,64,128]{2,1,0:T(8,128)(2,1)} %param.13) | copy-start | bytes 49156
  46.0 52.7 %copy-start.4 = (bf16[1,64,192]{2,1,0:T(8,128)(2,1)S(1)}, bf16[1,64,192]{2,1,0:T(8,128)(2,1)}, u32[]{:S(2)}) copy-start(bf16[1,64,192]{2,1,0:T(8,128)(2,1)} %param.12) | copy-start | bytes 73732
  48.0 71.0 %all-to-all-start = ((bf16[8,4,64,320]{3,2,1,0:T(8,128)(2,1)}), bf16[8,4,64,320]{3,2,1,0:T(8,128)(2,1)S(1)}, u32[]{:S(2)}, u32[]{:S(2)}) async-start(bf16[8,4,64,320]{3,2,1,0:T(8,128)(2,1)} %maximum_select_fusion), calls=%async_computation | async-start | bytes 3145728 | tf_op jit(solution)/shard_map/all_to_all | solution.py:94
  51.6 114.8 %reduce-scatter.4.cloned.1.call-start = ((), (), s32[]{:S(2)}) async-start(), calls=%async_computation.2 | async-start | bytes 819200
  98.8 15.9 %copy-start.1 = (bf16[128,16,192]{2,1,0:T(8,128)(2,1)}, bf16[128,16,192]{2,1,0:T(8,128)(2,1)S(1)}, u32[]{:S(2)}) copy-start(bf16[128,16,192]{2,1,0:T(8,128)(2,1)S(1)} %copy.34) | copy-start | bytes 2359300
  114.0 0.9 copy-start.3
  114.9 3.5 %copy-start.2 = (bf16[1,2560,32]{1,2,0:T(8,128)(2,1)S(1)}, bf16[1,2560,32]{1,2,0:T(8,128)(2,1)}, u32[]{:S(2)}) copy-start(bf16[1,2560,32]{1,2,0:T(8,128)(2,1)} %param.15) | copy-start | bytes 491524
  114.9 4.0 %copy-start.6 = (s32[1,1,16]{2,1,0:T(1,128)S(1)}, s32[1,1,16]{2,1,0:T(1,128)}, u32[]{:S(2)}) copy-start(s32[1,1,16]{2,1,0:T(1,128)} %param.17) | copy-start | bytes 196
Sparse Core Ops, SparseCore 0:
  139.9 26.4 reduce-scatter.3
